TPU v7x, 256 devices: a whole 4x4x8 slice. The times are simulated.
256 devices in a mesh: samp: 8 (over x, core), var: 32 (over z, y).
Axes of the slice: x: 4, y: 4, z: 8, core: 2. Of those that a mesh axis runs over, the one named last changes fastest.
Arguments:
- phenotype: bfloat16 [65536, 256], P(('samp', 'var')), may hold values from -1500 to 1500
- inverse_blocks: float32 [256, 256, 256], P(('samp', 'var')), may hold values from -1 to 2, as said below
- bin_sizes: int32 [8, 32], P('samp', 'var'), may hold values from 128 to 256, as said below
- slot_of: int32 [49152], P('samp'), may hold values from 0 to 8191, as said below
- dosages: bfloat16 [49152, 32768], P('samp', 'var'), may hold values from 0 to 2
Outputs:
- z_scores: float32 [32768, 256], P('var', 'samp')
Inputs may be any that keep to these rules, and one draw needn't show every extreme that they name: `bin_sizes`: within each row (one sample shard) the sizes sum to 192 times the row's length, and at least one bin is full. `slot_of`: within each sample shard the samples occupy exactly the live slots: slot v * 256 + r with r < bin_sizes of bin v, each once. `inverse_blocks`: each block is symmetric positive definite.
All inputs are finite; a program needn't handle non-finite values.
Results may differ from a plain program's by a relative error of at most 0.0041.
Values may be sent and summed in bfloat16 or wider, within the bound.
A program may use at most 128 MiB of HBM per device.

v0:
```python
import jax
import jax.numpy as jnp
from jax import lax
from jax.sharding import Mesh
from jax.sharding import PartitionSpec as P

SAMP_VAR = ("samp_0", "samp_1", "var_0", "var_1")
VAR = ("var_0", "var_1")
SAMP = ("samp_0", "samp_1")
epsilon = 1e-06


def one_axis_at_a_time(value, axes):
    for axis in axes:
        value = lax.psum(value, axis)
    return value


def gather_axes(value, axes, dim):
    if not axes:
        return value
    nearer = lax.all_gather(value, axes[-1], axis=dim, tiled=True)
    return gather_axes(nearer, axes[:-1], dim)


def in_blocks(value, dim, peers):
    before, after = (value.shape[:dim], value.shape[dim + 1 :])
    return jnp.moveaxis(value.reshape(*before, peers, -1, *after), dim, 0)


def sent_and_summed(value, axis, dim):
    peers = lax.axis_size(axis)
    pieces = lax.all_to_all(in_blocks(value, dim, peers), axis, 0, 0, tiled=True)
    return jnp.sum(pieces.astype(jnp.float32), axis=0)


def copy_for_each(value, axis):
    peers = lax.axis_size(axis)
    return lax.all_to_all(
        jnp.broadcast_to(value[None], (peers, *value.shape)), axis, 0, 0, tiled=True
    )


def taken_together(value, axis):
    return copy_for_each(value, axis).sum(axis=0)


def local(phenotype, inverse_blocks, bin_sizes, slot_of, dosages):
    bin_width = inverse_blocks.shape[1]
    position = jnp.arange(bin_width, dtype=jnp.int32)
    live_mask = (position < bin_sizes.reshape(())).astype(jnp.float32)[:, None]
    masked_pheno = phenotype.astype(jnp.float32) * live_mask
    whitened = (
        jnp.dot(
            inverse_blocks[0],
            masked_pheno,
            precision=lax.Precision.HIGHEST,
            preferred_element_type=jnp.float32,
        )
        * live_mask
    )
    trait_scale = one_axis_at_a_time(jnp.sum(masked_pheno * whitened, axis=0), SAMP_VAR)
    white_rows = whitened.astype(jnp.bfloat16)
    slot_weight = jnp.diagonal(inverse_blocks[0]).astype(jnp.bfloat16)
    gathered, weights_all = (gather_axes(white_rows, VAR, 0), gather_axes(slot_weight, VAR, 0))
    picked = jnp.take(gathered, slot_of, axis=0)
    score_part = lax.dot_general(
        dosages, picked, (((0,), (0,)), ((), ())), preferred_element_type=jnp.float32
    )
    sample_weight = jnp.take(weights_all, slot_of).astype(jnp.float32)
    variance = jnp.dot(
        sample_weight, dosages.astype(jnp.float32) ** 2, precision=lax.Precision.HIGHEST
    )
    trait_count = phenotype.shape[1] // lax.axis_size(SAMP)
    trait_start = lax.axis_index(SAMP) * trait_count
    score_share = sent_and_summed(score_part.astype(jnp.bfloat16), SAMP, 1)
    variance_all = taken_together(variance, SAMP)
    scale_share = lax.dynamic_slice_in_dim(trait_scale, trait_start, trait_count, 0)
    sample_count = slot_of.shape[0] * lax.axis_size(SAMP)
    return score_share / jnp.sqrt(
        variance_all[:, None] * scale_share[None, :] / sample_count + epsilon
    )


def solution(mesh):
    split = Mesh(mesh.devices.reshape(4, 2, 8, 4), ("samp_0", "samp_1", "var_0", "var_1"))
    in_specs = (P(SAMP_VAR, None), P(SAMP_VAR, None, None), P(SAMP, VAR), P(SAMP), P(SAMP, VAR))
    out_specs = P(VAR, SAMP)
    return jax.shard_map(local, mesh=split, in_specs=in_specs, out_specs=out_specs, check_vma=False)
```

profile of v0, /device:TPU:8, one launch (start us, length us, event | category | flops | bytes accessed | tf_op | source)
XLA Modules:
  0.0 200.2 jit_solution(13679015611097144882)
XLA Ops:
  7.2 0.3 copy-done
  7.5 1.5 multiply_reduce_fusion
  9.0 14.4 %all_gather.12 = bf16[1024,256]{1,0:T(8,128)(2,1)} all-gather(bf16[256,256]{1,0:T(8,128)(2,1)S(1)} %get-tuple-element.8), channel_id=1, replica_groups=mesh['samp_0'=4,'samp_1'=2,'var_0'=8,'var_1'=4] {'var_1'}, dimensions={0}, use_global_device_ids=true | all-gather | bytes 655360 | tf_op jit(solution)/shard_map/all_gather | solution.py:22
  23.4 0.0 all-gather.3.cloned.1.call-update
  23.4 2.3 %gather_fusion.1 = bf16[256]{0:T(256)(128)(2,1)S(1)} fusion(f32[256,256]{1,0:T(8,128)S(1)} %bitcast.20, s32[256]{0:T(256)S(1)} %bitcast.21), kind=kCustom, calls=%fused_computation.1 | custom fusion | bytes 3072 | tf_op jit(solution)/shard_map/jit(diagonal)/cond/branch_0_fun/gather | solution.py:64
  25.8 8.5 %all-gather = bf16[4,1,256]{2,1,0:T(2,128)(2,1)S(1)} all-gather(bf16[1,1,256]{2,1,0:T(2,128)(2,1)S(1)} %reshape.50), channel_id=1, replica_groups=mesh['samp_0'=4,'samp_1'=2,'var_0'=8,'var_1'=4] {'var_1'}, dimensions={0}, use_global_device_ids=true | all-gather | bytes 2560 | tf_op jit(solution)/shard_map/all_gather | solution.py:22
  34.4 24.0 %all_gather.15 = bf16[8192]{0:T(1024)(128)(2,1)S(1)} all-gather(bf16[1024]{0:T(1024)(128)(2,1)S(1)} %bitcast.24), channel_id=1, replica_groups=mesh['samp_0'=4,'samp_1'=2,'var_0'=8,'var_1'=4] {'var_0'}, dimensions={0}, use_global_device_ids=true | all-gather | bytes 18432 | tf_op jit(solution)/shard_map/all_gather | solution.py:22
  58.4 0.7 fusion.12
  59.1 0.0 copy-start.1
  59.1 38.2 %gather_fusion.2 = bf16[6144]{0:T(1024)(128)(2,1)S(1)} fusion(bf16[8192]{0:T(1024)(128)(2,1)S(1)} %all_gather.15, s32[6144]{0:T(1024)S(1)} %fusion.12), kind=kCustom, calls=%fused_computation.2 | custom fusion | bytes 49152 | tf_op jit(solution)/shard_map/jit(_take)/gather | solution.py:70
  97.4 12.3 %fusion = f32[1,1024]{1,0:T(1,128)S(1)} fusion(bf16[6144,1]{0,1:T(2,128)(2,1)S(1)} %reshape.52, bf16[6144,1024]{1,0:T(8,128)(2,1)} %param.9), kind=kOutput, calls=%fused_computation.3 | convolution fusion | flops 88080384 | bytes 12599296 | tf_op jit(solution)/shard_map/dot_general | solution.py:71
  109.7 0.6 broadcast_in_dim.35
  110.3 4.3 %all-to-all-start.1 = ((f32[8,1,1024]{2,1,0:T(1,128)}), f32[8,1,1024]{2,1,0:T(1,128)S(1)}, u32[]{:S(2)}, u32[]{:S(2)}) async-start(f32[8,1,1024]{2,1,0:T(1,128)} %broadcast_in_dim.35), calls=%async_computation.1 | async-start | bytes 65536 | tf_op jit(solution)/shard_map/all_to_all | solution.py:39
  114.6 0.0 all-gather.3.cloned.1.call-done
  114.6 22.1 %gather_fusion = bf16[6144,256]{1,0:T(8,128)(2,1)S(1)} fusion(bf16[8192,256]{1,0:T(8,128)(2,1)} %all-gather.3.cloned.1.call-done, s32[6144]{0:T(1024)S(1)} %fusion.12), kind=kCustom, calls=%fused_computation | custom fusion | bytes 6316032 | tf_op jit(solution)/shard_map/jit(_take)/gather | solution.py:66
  136.7 9.7 %fusion.7 = bf16[256,1024]{1,0:T(8,128)(2,1)} fusion(bf16[6144,1024]{1,0:T(8,128)(2,1)} %param.9, bf16[6144,256]{1,0:T(8,128)(2,1)S(1)} %gather_fusion, pred[6144]{0:T(1024)(128)(4,1)S(1)} %get-tuple-element.6), kind=kOutput, calls=%fused_computation.10 | convolution fusion | flops 3223060480 | bytes 16259072 | tf_op jit(solution)/shard_map/dot_general | solution.py:67
  146.4 4.8 %all-to-all-start = ((bf16[8,1024,32]{1,2,0:T(8,128)(2,1)}), bf16[8,1024,32]{1,2,0:T(8,128)(2,1)S(1)}, u32[]{:S(2)}, u32[]{:S(2)}) async-start(bf16[8,1024,32]{1,2,0:T(8,128)(2,1)} %bitcast.22), calls=%async_computation | async-start | bytes 1048576 | tf_op jit(solution)/shard_map/all_to_all | solution.py:33
  151.2 12.6 %psum.28 = f32[256]{0:T(256)S(1)} all-reduce(f32[256]{0:T(256)S(1)} %get-tuple-element.7), channel_id=1, replica_groups=mesh['samp_0'=4,'samp_1'=2,'var_0'=8,'var_1'=4] {'samp_0'}, use_global_device_ids=true, to_apply=%region_3.0 | all-reduce | flops 256 | bytes 2048 | tf_op jit(solution)/shard_map/psum | solution.py:15
  163.8 2.4 %psum.29 = f32[256]{0:T(256)S(1)} all-reduce(f32[256]{0:T(256)S(1)} %psum.28), channel_id=1, replica_groups=mesh['samp_0'=4,'samp_1'=2,'var_0'=8,'var_1'=4] {'samp_1'}, use_global_device_ids=true, to_apply=%region_4.0 | all-reduce | flops 256 | bytes 2048 | tf_op jit(solution)/shard_map/psum | solution.py:15
  166.2 15.4 %psum.30 = f32[256]{0:T(256)S(1)} all-reduce(f32[256]{0:T(256)S(1)} %psum.29), channel_id=1, replica_groups=mesh['samp_0'=4,'samp_1'=2,'var_0'=8,'var_1'=4] {'var_0'}, use_global_device_ids=true, to_apply=%region_5.6 | all-reduce | flops 256 | bytes 2048 | tf_op jit(solution)/shard_map/psum | solution.py:15
  181.6 10.8 %psum.31 = f32[256]{0:T(256)S(1)} all-reduce(f32[256]{0:T(256)S(1)} %psum.30), channel_id=1, replica_groups=mesh['samp_0'=4,'samp_1'=2,'var_0'=8,'var_1'=4] {'var_1'}, use_global_device_ids=true, to_apply=%region_6.7 | all-reduce | flops 256 | bytes 2048 | tf_op jit(solution)/shard_map/psum | solution.py:15
  192.4 0.1 dynamic_slice.3
  192.5 0.1 convert_reduce_fusion
  192.6 0.8 rsqrt_multiply_fusion
  (13 shorter events, 0.1 us)
Async XLA Ops:
  6.5 1.0 copy-start
  6.5 108.1 %all-gather.3.cloned.1.call-start = ((), (), s32[]{:S(2)}) async-start(), calls=%async_computation.2 | async-start | bytes 4718592 | tf_op jit(solution)/shard_map/all_gather | solution.py:22
  59.1 38.2 %copy-start.1 = (s32[6144]{0:T(1024)S(1)}, s32[6144]{0:T(1024)}, u32[]{:S(2)}) copy-start(s32[6144]{0:T(1024)} %param.8) | copy-start | bytes 73732
  110.3 36.1 %all-to-all-start.1 = ((f32[8,1,1024]{2,1,0:T(1,128)}), f32[8,1,1024]{2,1,0:T(1,128)S(1)}, u32[]{:S(2)}, u32[]{:S(2)}) async-start(f32[8,1,1024]{2,1,0:T(1,128)} %broadcast_in_dim.35), calls=%async_computation.1 | async-start | bytes 65536 | tf_op jit(solution)/shard_map/all_to_all | solution.py:39
  146.4 46.1 %all-to-all-start = ((bf16[8,1024,32]{1,2,0:T(8,128)(2,1)}), bf16[8,1024,32]{1,2,0:T(8,128)(2,1)S(1)}, u32[]{:S(2)}, u32[]{:S(2)}) async-start(bf16[8,1024,32]{1,2,0:T(8,128)(2,1)} %bitcast.22), calls=%async_computation | async-start | bytes 1048576 | tf_op jit(solution)/shard_map/all_to_all | solution.py:33
Sparse Core Ops, SparseCore 0:
  23.5 57.5 all-gather.2
where the time goes:
time: 201 us; the launch traced here: 200 us
  blocking collectives  88.2 us (44%)
  local copies, waits for them, and re-layouts  63.6 us (32%)
  matrix products  23.4 us (12%)
  between operations  14.2 us (7%)
  starting transfers between devices  9.07 us (5%)
    all_gather x3, blocking collectives, gather_axes(): nearer = lax.all_gather(value, axes[-1], axis=dim, tiled=True)  47 us
    psum x4, blocking collectives, one_axis_at_a_time(): value = lax.psum(value, axis)  41.3 us
    gather x1, local copies, waits for them, and re-layouts, local(): sample_weight = jnp.take(weights_all, slot_of).astype(jnp.float32)  38.2 us
    gather x1, local copies, waits for them, and re-layouts, local(): picked = jnp.take(gathered, slot_of, axis=0)  22.1 us
    dot_general x1, matrix products, local(): jnp.dot(sample_weight, dosages.astype(jnp.float32) ** 2, precision=lax.Pr...  12.3 us
    dot_general x1, matrix products, local(): lax.dot_general(dosages, picked, (((0,), (0,)), ((), ())), preferred_elem...  9.66 us
    all_to_all x1, starting transfers between devices, sent_and_summed(): lax.all_to_all(in_blocks(value, dim, peers), axis, 0, 0, tiled=True)  4.78 us
    all_to_all x1, starting transfers between devices, copy_for_each(): lax.all_to_all(jnp.broadcast_to(value[None], (peers, *value.shape)), axis...  4.29 us
  transfers between devices with their start and end apart: 3, of which 0 were waited for; matrix products, arithmetic and copies ran while one was open for 43% of the time, Pallas kernels for 0%

commit v1 on v0

--- a/solution.py
+++ b/solution.py
@@ -12,7 +12,7 @@
 
 def one_axis_at_a_time(value, axes):
     for axis in axes:
-        value = lax.psum(value, axis)
+        value = jax.lax.all_gather(value, axis_name=axis).sum(axis=0)
     return value
 
 

time: 201 us -> 198 us (0.985)
  blocking collectives: 88.2 us -> 85.8 us
    psum x4 -> x0, blocking collectives: 41.3 us -> none  [one_axis_at_a_time(): value = lax.psum(value, axis)]
    all_gather x0 -> x4, blocking collectives: none -> 38.9 us  [one_axis_at_a_time(): value = jax.lax.all_gather(value, axis_name=axis).sum(axis=0)]
  transfers between devices with their start and end apart: 3 -> 3, of which waited for: 0 -> 0; matrix products, arithmetic and copies ran while one was open for 43% -> 44% of each run, Pallas kernels for 0% -> 0%
where the time goes in v1:
time: 198 us
  blocking collectives  85.8 us (43%)
  local copies, waits for them, and re-layouts  63.6 us (32%)
  matrix products  23.4 us (12%)
  between operations  14.2 us (7%)
  starting transfers between devices  9.07 us (5%)
    all_gather x3, blocking collectives, gather_axes(): nearer = lax.all_gather(value, axes[-1], axis=dim, tiled=True)  47 us
    all_gather x4, blocking collectives, one_axis_at_a_time(): value = jax.lax.all_gather(value, axis_name=axis).sum(axis=0)  38.9 us
    gather x1, local copies, waits for them, and re-layouts, local(): sample_weight = jnp.take(weights_all, slot_of).astype(jnp.float32)  38.2 us
    gather x1, local copies, waits for them, and re-layouts, local(): picked = jnp.take(gathered, slot_of, axis=0)  22.1 us
    dot_general x1, matrix products, local(): jnp.dot(sample_weight, dosages.astype(jnp.float32) ** 2, precision=lax.Pr...  12.3 us
    dot_general x1, matrix products, local(): lax.dot_general(dosages, picked, (((0,), (0,)), ((), ())), preferred_elem...  9.66 us
    all_to_all x1, starting transfers between devices, sent_and_summed(): lax.all_to_all(in_blocks(value, dim, peers), axis, 0, 0, tiled=True)  4.78 us
    all_to_all x1, starting transfers between devices, copy_for_each(): lax.all_to_all(jnp.broadcast_to(value[None], (peers, *value.shape)), axis...  4.29 us
  transfers between devices with their start and end apart: 3, of which 0 were waited for; matrix products, arithmetic and copies ran while one was open for 44% of the time, Pallas kernels for 0%

profile of v1, /device:TPU:8, one launch (start us, length us, event | category | flops | bytes accessed | tf_op | source)
XLA Modules:
  0.0 197.9 jit_solution(5238973402900472335)
XLA Ops:
  7.2 0.3 copy-done
  7.5 1.5 multiply_reduce_fusion
  9.0 14.4 %all_gather.36 = bf16[1024,256]{1,0:T(8,128)(2,1)} all-gather(bf16[256,256]{1,0:T(8,128)(2,1)S(1)} %get-tuple-element.8), channel_id=1, replica_groups=mesh['samp_0'=4,'samp_1'=2,'var_0'=8,'var_1'=4] {'var_1'}, dimensions={0}, use_global_device_ids=true | all-gather | bytes 655360 | tf_op jit(solution)/shard_map/all_gather | solution.py:22
  23.4 0.0 all-gather.11.cloned.1.call-update
  23.4 2.3 %gather_fusion.1 = bf16[256]{0:T(256)(128)(2,1)S(1)} fusion(f32[256,256]{1,0:T(8,128)S(1)} %bitcast.24, s32[256]{0:T(256)S(1)} %bitcast.25), kind=kCustom, calls=%fused_computation.1 | custom fusion | bytes 3072 | tf_op jit(solution)/shard_map/jit(diagonal)/cond/branch_0_fun/gather | solution.py:64
  25.8 8.5 %all-gather.4 = bf16[4,1,256]{2,1,0:T(2,128)(2,1)S(1)} all-gather(bf16[1,1,256]{2,1,0:T(2,128)(2,1)S(1)} %reshape.54), channel_id=1, replica_groups=mesh['samp_0'=4,'samp_1'=2,'var_0'=8,'var_1'=4] {'var_1'}, dimensions={0}, use_global_device_ids=true | all-gather | bytes 2560 | tf_op jit(solution)/shard_map/all_gather | solution.py:22
  34.4 24.0 %all_gather.39 = bf16[8192]{0:T(1024)(128)(2,1)S(1)} all-gather(bf16[1024]{0:T(1024)(128)(2,1)S(1)} %bitcast.28), channel_id=1, replica_groups=mesh['samp_0'=4,'samp_1'=2,'var_0'=8,'var_1'=4] {'var_0'}, dimensions={0}, use_global_device_ids=true | all-gather | bytes 18432 | tf_op jit(solution)/shard_map/all_gather | solution.py:22
  58.4 0.7 fusion.12
  59.1 0.0 copy-start.1
  59.1 38.2 %gather_fusion.2 = bf16[6144]{0:T(1024)(128)(2,1)S(1)} fusion(bf16[8192]{0:T(1024)(128)(2,1)S(1)} %all_gather.39, s32[6144]{0:T(1024)S(1)} %fusion.12), kind=kCustom, calls=%fused_computation.2 | custom fusion | bytes 49152 | tf_op jit(solution)/shard_map/jit(_take)/gather | solution.py:70
  97.4 12.3 %fusion = f32[1,1024]{1,0:T(1,128)S(1)} fusion(bf16[6144,1]{0,1:T(2,128)(2,1)S(1)} %reshape.68, bf16[6144,1024]{1,0:T(8,128)(2,1)} %param.9), kind=kOutput, calls=%fused_computation.3 | convolution fusion | flops 88080384 | bytes 12599296 | tf_op jit(solution)/shard_map/dot_general | solution.py:71
  109.7 0.6 broadcast_in_dim.35
  110.3 4.3 %all-to-all-start.1 = ((f32[8,1,1024]{2,1,0:T(1,128)}), f32[8,1,1024]{2,1,0:T(1,128)S(1)}, u32[]{:S(2)}, u32[]{:S(2)}) async-start(f32[8,1,1024]{2,1,0:T(1,128)} %broadcast_in_dim.35), calls=%async_computation.1 | async-start | bytes 65536 | tf_op jit(solution)/shard_map/all_to_all | solution.py:39
  114.6 0.0 all-gather.11.cloned.1.call-done
  114.6 22.1 %gather_fusion = bf16[6144,256]{1,0:T(8,128)(2,1)S(1)} fusion(bf16[8192,256]{1,0:T(8,128)(2,1)} %all-gather.11.cloned.1.call-done, s32[6144]{0:T(1024)S(1)} %fusion.12), kind=kCustom, calls=%fused_computation | custom fusion | bytes 6316032 | tf_op jit(solution)/shard_map/jit(_take)/gather | solution.py:66
  136.7 9.7 %fusion.7 = bf16[256,1024]{1,0:T(8,128)(2,1)} fusion(bf16[6144,1024]{1,0:T(8,128)(2,1)} %param.9, bf16[6144,256]{1,0:T(8,128)(2,1)S(1)} %gather_fusion, pred[6144]{0:T(1024)(128)(4,1)S(1)} %get-tuple-element.6), kind=kOutput, calls=%fused_computation.10 | convolution fusion | flops 3223060480 | bytes 16259072 | tf_op jit(solution)/shard_map/dot_general | solution.py:67
  146.4 4.8 %all-to-all-start = ((bf16[8,1024,32]{1,2,0:T(8,128)(2,1)}), bf16[8,1024,32]{1,2,0:T(8,128)(2,1)S(1)}, u32[]{:S(2)}, u32[]{:S(2)}) async-start(bf16[8,1024,32]{1,2,0:T(8,128)(2,1)} %bitcast.26), calls=%async_computation | async-start | bytes 1048576 | tf_op jit(solution)/shard_map/all_to_all | solution.py:33
  151.2 12.5 %all-gather.5 = f32[4,1,256]{2,1,0:T(1,128)S(1)} all-gather(f32[1,1,256]{2,1,0:T(1,128)S(1)} %bitcast.30), channel_id=2, replica_groups=mesh['samp_0'=4,'samp_1'=2,'var_0'=8,'var_1'=4] {'samp_0'}, dimensions={0}, use_global_device_ids=true | all-gather | bytes 5120 | tf_op jit(solution)/shard_map/all_gather | solution.py:15
  163.7 1.8 all-gather.6
  165.5 14.5 %all-gather.7 = f32[8,1,256]{2,1,0:T(1,128)S(1)} all-gather(f32[1,1,256]{2,1,0:T(1,128)S(1)} %bitcast.31), channel_id=4, replica_groups=mesh['samp_0'=4,'samp_1'=2,'var_0'=8,'var_1'=4] {'var_0'}, dimensions={0}, use_global_device_ids=true | all-gather | bytes 9216 | tf_op jit(solution)/shard_map/all_gather | solution.py:15
  180.0 10.1 %all-gather.8 = f32[4,1,256]{2,1,0:T(1,128)S(1)} all-gather(f32[1,1,256]{2,1,0:T(1,128)S(1)} %bitcast.32), channel_id=5, replica_groups=mesh['samp_0'=4,'samp_1'=2,'var_0'=8,'var_1'=4] {'var_1'}, dimensions={0}, use_global_device_ids=true | all-gather | bytes 5120 | tf_op jit(solution)/shard_map/all_gather | solution.py:15
  190.1 0.1 dynamic_slice.3
  190.2 0.1 convert_reduce_fusion
  190.3 0.8 rsqrt_multiply_fusion
  (17 shorter events, 0.2 us)
Async XLA Ops:
  6.5 1.0 copy-start
  6.5 108.1 %all-gather.11.cloned.1.call-start = ((), (), s32[]{:S(2)}) async-start(), calls=%async_computation.2 | async-start | bytes 4718592 | tf_op jit(solution)/shard_map/all_gather | solution.py:22
  59.1 38.2 %copy-start.1 = (s32[6144]{0:T(1024)S(1)}, s32[6144]{0:T(1024)}, u32[]{:S(2)}) copy-start(s32[6144]{0:T(1024)} %param.8) | copy-start | bytes 73732
  110.3 36.1 %all-to-all-start.1 = ((f32[8,1,1024]{2,1,0:T(1,128)}), f32[8,1,1024]{2,1,0:T(1,128)S(1)}, u32[]{:S(2)}, u32[]{:S(2)}) async-start(f32[8,1,1024]{2,1,0:T(1,128)} %broadcast_in_dim.35), calls=%async_computation.1 | async-start | bytes 65536 | tf_op jit(solution)/shard_map/all_to_all | solution.py:39
  146.4 43.8 %all-to-all-start = ((bf16[8,1024,32]{1,2,0:T(8,128)(2,1)}), bf16[8,1024,32]{1,2,0:T(8,128)(2,1)S(1)}, u32[]{:S(2)}, u32[]{:S(2)}) async-start(bf16[8,1024,32]{1,2,0:T(8,128)(2,1)} %bitcast.26), calls=%async_computation | async-start | bytes 1048576 | tf_op jit(solution)/shard_map/all_to_all | solution.py:33
Sparse Core Ops, SparseCore 0:
  23.5 57.5 all-gather.10
